TPU v7x, 512 devices: a whole 4x8x8 slice. The times are simulated.
512 devices in a mesh: expert: 128 (over z, y, core), etp: 4 (over x).
Axes of the slice: x: 4, y: 8, z: 8, core: 2. Of those that a mesh axis runs over, the one named last changes fastest.
Arguments:
- tokens: bfloat16 [16384, 2048], P('expert', 'etp'), may hold values from -6 to 6
- out_grad: bfloat16 [16384, 2048], P('expert', 'etp'), may hold values from -12 to 12
- routes: int32 [16384, 8], P('expert'), may hold values from 0 to 127, all different within a row; in each aligned block of 128 rows (0 to 127, 128 to 255, ...) at most 9 rows name the same one
- combine: float32 [16384, 8], P('expert'), may hold values from 0.02 to 0.5
- w_gate: bfloat16 [128, 768, 2048], P('expert', 'etp'), may hold values from -0.125 to 0.125
- w_up: bfloat16 [128, 768, 2048], P('expert', 'etp'), may hold values from -0.125 to 0.125
- w_down: bfloat16 [128, 768, 2048], P('expert', 'etp'), may hold values from -0.21875 to 0.21875
Outputs:
- grad_tokens: bfloat16 [16384, 2048], P('expert', 'etp')
- grad_gate: bfloat16 [128, 768, 2048], P('expert', 'etp')
- grad_up: bfloat16 [128, 768, 2048], P('expert', 'etp')
- grad_down: bfloat16 [128, 768, 2048], P('expert', 'etp')
Inputs may be any that keep to these rules, and one draw needn't show every extreme that they name: `routes`: each row names 8 different experts. Within each aligned block of 128 rows (the rows of one index of expert) no expert is named by more than 9 rows, and in some block one expert is named by exactly 9 rows.
All inputs are finite; a program needn't handle non-finite values.
Results may differ from a plain program's by a relative error of at most 0.0064.
Values may be sent and summed in bfloat16 or wider, within the bound.
A program may use at most 128 MiB of HBM per device.

v0:
```python
import jax
import jax.numpy as jnp
from jax import lax
from jax.sharding import PartitionSpec as P


def pack_rows(token_rows, grad_rows, token_of, scale, is_live):
    mask = is_live[:, None].astype(token_rows.dtype)
    inputs_sent = token_rows[token_of] * mask
    grads_sent = (scale[:, None] * grad_rows[token_of].astype(jnp.float32)).astype(jnp.bfloat16)
    return (inputs_sent, grads_sent)


def pair_positions(routed_flat, experts):
    pair_total = routed_flat.shape[0]
    span = 128
    groups = pair_total // span
    labels = jnp.arange(experts, dtype=jnp.int32)
    one_hot = (routed_flat[:, None] == labels[None, :]).astype(jnp.bfloat16)
    grouped = one_hot.reshape(groups, span, experts)
    row_ids = jnp.arange(span, dtype=jnp.int32)
    lower = (row_ids[None, :] < row_ids[:, None]).astype(jnp.bfloat16)
    within = jnp.einsum("ij,bje->bie", lower, grouped, preferred_element_type=jnp.float32)
    group_sums = jnp.sum(grouped.astype(jnp.float32), axis=1)
    group_before = jnp.cumsum(group_sums, axis=0) - group_sums
    earlier = within + group_before[:, None, :]
    counted = jnp.sum(earlier * grouped.astype(jnp.float32), axis=2)
    return counted.reshape(pair_total).astype(jnp.int32)


def body(tokens, out_grad, routes, combine, w_gate, w_up, w_down):
    experts = lax.axis_size("expert")
    tok_rows = tokens.shape[0]
    col_width = tokens.shape[1]
    choose_count = routes.shape[1]
    per_pair = tok_rows * choose_count // experts
    capacity = per_pair + per_pair // 8
    routed_flat = routes.reshape(-1)
    pair_total = routed_flat.shape[0]
    position = pair_positions(routed_flat, experts)
    target = routed_flat * capacity + position
    anchor = jnp.full((experts * capacity,), pair_total, jnp.int32)
    anchor = anchor.at[target].set(jnp.arange(pair_total, dtype=jnp.int32))
    is_live = anchor < pair_total
    safe_anchor = jnp.minimum(anchor, pair_total - 1)
    token_of = safe_anchor // choose_count
    scale = combine.reshape(-1)[safe_anchor] * is_live.astype(jnp.float32)
    full_tokens, full_grads = (
        lax.all_gather(tokens, "etp", axis=1, tiled=True),
        lax.all_gather(out_grad, "etp", axis=1, tiled=True),
    )
    inputs_sent, grads_sent = pack_rows(full_tokens, full_grads, token_of, scale, is_live)
    rows_x, rows_g = (
        lax.all_to_all(inputs_sent, "expert", split_axis=0, concat_axis=0, tiled=True),
        lax.all_to_all(grads_sent, "expert", split_axis=0, concat_axis=0, tiled=True),
    )
    gate_w = w_gate[0]
    up_w = w_up[0]
    down_w = w_down[0]
    contract_last = (((1,), (1,)), ((), ()))
    contract_first = (((0,), (0,)), ((), ()))
    gate = lax.dot_general(rows_x, gate_w, contract_last, preferred_element_type=jnp.float32)
    up = lax.dot_general(rows_x, up_w, contract_last, preferred_element_type=jnp.float32)
    hidden_grad = lax.dot_general(rows_g, down_w, contract_last, preferred_element_type=jnp.float32)
    sigma = jax.nn.sigmoid(gate)
    silu = gate * sigma
    acts = (silu * up).astype(jnp.bfloat16)
    grad_down = lax.dot_general(acts, rows_g, contract_first, preferred_element_type=jnp.float32)
    gate_term = (hidden_grad * up * sigma * (1.0 + gate * (1.0 - sigma))).astype(jnp.bfloat16)
    up_term = (hidden_grad * silu).astype(jnp.bfloat16)
    grad_gate = lax.dot_general(
        gate_term, rows_x, contract_first, preferred_element_type=jnp.float32
    )
    grad_up = lax.dot_general(up_term, rows_x, contract_first, preferred_element_type=jnp.float32)
    swapped_gate, swapped_up = (
        lax.all_to_all(gate_w, "etp", split_axis=1, concat_axis=0, tiled=True),
        lax.all_to_all(up_w, "etp", split_axis=1, concat_axis=0, tiled=True),
    )
    running = jnp.dot(
        lax.all_gather(gate_term, "etp", axis=1, tiled=True),
        swapped_gate,
        preferred_element_type=jnp.float32,
    )
    slot_grads = running + jnp.dot(
        lax.all_gather(up_term, "etp", axis=1, tiled=True),
        swapped_up,
        preferred_element_type=jnp.float32,
    )
    slot_grads = slot_grads.astype(jnp.bfloat16)
    returned = lax.all_to_all(slot_grads, "expert", split_axis=0, concat_axis=0, tiled=True)
    picked = returned[target].astype(jnp.float32).reshape(tok_rows, choose_count, col_width)
    grad_tokens = jnp.sum(picked, axis=1).astype(jnp.bfloat16)
    return (
        grad_tokens,
        grad_gate.astype(jnp.bfloat16)[None],
        grad_up.astype(jnp.bfloat16)[None],
        grad_down.astype(jnp.bfloat16)[None],
    )


def solution(mesh):
    placed = (
        P("expert", "etp"),
        P("expert", "etp"),
        P("expert", None),
        P("expert", None),
        P("expert", "etp", None),
        P("expert", "etp", None),
        P("expert", "etp", None),
    )
    return jax.shard_map(
        body,
        mesh=mesh,
        in_specs=placed,
        out_specs=(
            P("expert", "etp"),
            P("expert", "etp", None),
            P("expert", "etp", None),
            P("expert", "etp", None),
        ),
        check_vma=False,
    )
```

profile of v0, /device:TPU:1, one launch (start us, length us, event | category | flops | bytes accessed | tf_op | source)
XLA Modules:
  0.0 754.0 jit_solution(5431295311087049603)
XLA Ops:
  7.2 0.0 copy-start
  7.2 0.9 copy.20
  8.0 0.7 broadcast_multiply_fusion.1
  8.7 0.1 eq.17
  8.8 0.1 convert_reduce_fusion
  9.0 0.0 copy-start.6
  9.0 0.3 fusion.6
  9.3 0.1 copy.19
  9.4 0.1 mul.69
  9.5 4.3 scatter_custom_fusion
  13.9 0.8 copy.21
  14.7 0.1 reshape.109
  14.8 4.6 gather_fusion
  19.4 0.2 reshape.111
  19.6 0.0 copy-done.6
  19.6 11.1 %all_gather.13 = bf16[128,2048]{1,0:T(8,128)(2,1)S(1)} all-gather(bf16[128,512]{1,0:T(8,128)(2,1)S(1)} %copy-done.6), channel_id=1, replica_groups=mesh['expert'=128,'etp'=4] {'etp'}, dimensions={1}, use_global_device_ids=true | all-gather | bytes 655360 | tf_op jit(solution)/shard_map/all_gather | solution.py:49
  30.7 5.9 gather_fusion.2
  36.6 8.1 %gather.19 = bf16[128,9,2048]{2,1,0:T(8,128)(2,1)} reshape(bf16[1152,2048]{1,0:T(8,128)(2,1)} %gather_fusion.2) | data formatting | bytes 9437184 | tf_op jit(solution)/shard_map/gather | solution.py:9
  44.7 7.2 broadcast_multiply_fusion
  51.9 21.1 %all-to-all-start.1 = ((bf16[128,9,2048]{2,1,0:T(8,128)(2,1)}), bf16[128,9,2048]{2,1,0:T(8,128)(2,1)}, u32[]{:S(2)}, u32[]{:S(2)}) async-start(bf16[128,9,2048]{2,1,0:T(8,128)(2,1)} %broadcast_multiply_fusion), calls=%async_computation.1 | async-start | bytes 16777216 | tf_op jit(solution)/shard_map/all_to_all | solution.py:54
  73.0 0.2 mul.72
  73.2 11.9 %all_gather.12 = bf16[128,2048]{1,0:T(8,128)(2,1)S(1)} all-gather(bf16[128,512]{1,0:T(8,128)(2,1)S(1)} %copy-done.7), channel_id=1, replica_groups=mesh['expert'=128,'etp'=4] {'etp'}, dimensions={1}, use_global_device_ids=true | all-gather | bytes 655360 | tf_op jit(solution)/shard_map/all_gather | solution.py:50
  85.1 6.0 gather_fusion.1
  91.2 9.3 %reshape.110 = f32[128,9,2048]{2,1,0:T(8,128)} reshape(bf16[1152,2048]{1,0:T(8,128)(2,1)} %gather_fusion.1) | data formatting | bytes 14155776 | tf_op jit(solution)/shard_map/convert_element_type | solution.py:10
  100.5 9.0 %multiply_convert_fusion = bf16[128,9,2048]{2,1,0:T(8,128)(2,1)} fusion(f32[128,9,2048]{2,1,0:T(8,128)} %reshape.110, f32[128,9]{1,0:T(8,128)S(1)} %mul.72), kind=kLoop, calls=%fused_computation.5 | loop fusion | flops 4718592 | bytes 14160384 | tf_op jit(solution)/shard_map/convert_element_type | solution.py:10
  109.5 174.6 %all-to-all-done.1 = bf16[128,9,2048]{2,1,0:T(8,128)(2,1)} async-done(((bf16[128,9,2048]{2,1,0:T(8,128)(2,1)}), bf16[128,9,2048]{2,1,0:T(8,128)(2,1)}, u32[]{:S(2)}, u32[]{:S(2)}) %all-to-all-start.1) | async-done | bytes 4718624 | tf_op jit(solution)/shard_map/all_to_all | solution.py:54
  284.1 48.0 %all-to-all-start = ((bf16[128,9,2048]{2,1,0:T(8,128)(2,1)}), bf16[128,9,2048]{2,1,0:T(8,128)(2,1)}, u32[]{:S(2)}, u32[]{:S(2)}) async-start(bf16[128,9,2048]{2,1,0:T(8,128)(2,1)} %multiply_convert_fusion), calls=%async_computation | async-start | bytes 16777216 | tf_op jit(solution)/shard_map/all_to_all | solution.py:55
  332.1 0.0 copy-start.3
  332.2 0.2 all-gather.3.cloned.1.call-start
  332.4 8.4 %all_to_all.51 = bf16[1152,2048]{1,0:T(8,128)(2,1)} reshape(bf16[128,9,2048]{2,1,0:T(8,128)(2,1)} %all-to-all-done.1) | data formatting | bytes 9437184 | tf_op jit(solution)/shard_map/all_to_all | solution.py:54
  340.8 5.1 fusion.10
  346.0 2.7 fusion.8
  348.6 194.6 %all-to-all-done = bf16[128,9,2048]{2,1,0:T(8,128)(2,1)} async-done(((bf16[128,9,2048]{2,1,0:T(8,128)(2,1)}), bf16[128,9,2048]{2,1,0:T(8,128)(2,1)}, u32[]{:S(2)}, u32[]{:S(2)}) %all-to-all-start) | async-done | bytes 4718624 | tf_op jit(solution)/shard_map/all_to_all | solution.py:55
  543.2 8.5 %all_to_all.49 = bf16[1152,2048]{1,0:T(8,128)(2,1)} reshape(bf16[128,9,2048]{2,1,0:T(8,128)(2,1)} %all-to-all-done) | data formatting | bytes 9437184 | tf_op jit(solution)/shard_map/all_to_all | solution.py:55
  551.7 0.0 copy-done
  551.7 5.5 multiply_convert_fusion.2
  557.3 0.0 all-gather.3.cloned.1.call-update
  557.3 0.0 all-gather.5.cloned.1.call-start
  557.3 0.7 all-gather.5.cloned.1.call-update
  558.0 0.6 all_to_all.52
  558.6 1.0 copy.22
  559.6 4.0 all-to-all-start.2
  563.6 0.6 all_to_all.56
  564.2 1.0 copy.23
  565.2 6.7 all-to-all-done.2
  572.0 3.5 all-to-all-start.3
  575.5 49.8 %all-gather.3.cloned.1.call-done = bf16[1152,768]{0,1:T(8,128)(2,1)} async-done(((bf16[1152,192]{0,1:T(8,128)(2,1)}), bf16[1152,768]{0,1:T(8,128)(2,1)}) %all-gather.3.cloned.1.call-update) | async-done | bytes 1769488 | tf_op jit(solution)/shard_map/all_gather | solution.py:80
  625.3 4.0 fusion.24
  629.3 0.0 all-to-all-done.3
  629.3 39.1 %all-gather.5.cloned.1.call-done = bf16[1152,768]{0,1:T(8,128)(2,1)} async-done(((bf16[1152,192]{0,1:T(8,128)(2,1)}), bf16[1152,768]{0,1:T(8,128)(2,1)}) %all-gather.5.cloned.1.call-update) | async-done | bytes 1769488 | tf_op jit(solution)/shard_map/all_gather | solution.py:85
  668.4 3.3 fusion
  671.7 0.0 copy-start.5
  671.8 1.6 all_to_all.60
  673.3 15.1 %all-to-all-start.4 = ((bf16[128,9,512]{2,1,0:T(8,128)(2,1)}), bf16[128,9,512]{2,1,0:T(8,128)(2,1)}, u32[]{:S(2)}, u32[]{:S(2)}) async-start(bf16[128,9,512]{2,1,0:T(8,128)(2,1)} %all_to_all.60), calls=%async_computation.4 | async-start | bytes 4194304 | tf_op jit(solution)/shard_map/all_to_all | solution.py:90
  688.4 0.0 slice-start
  688.4 0.0 slice-start.1
  688.4 0.0 copy-start.8
  688.4 4.6 fusion.2
  693.0 4.4 fusion.1
  697.4 2.1 fusion.3
  699.6 39.7 %all-to-all-done.4 = bf16[128,9,512]{2,1,0:T(8,128)(2,1)} async-done(((bf16[128,9,512]{2,1,0:T(8,128)(2,1)}), bf16[128,9,512]{2,1,0:T(8,128)(2,1)}, u32[]{:S(2)}, u32[]{:S(2)}) %all-to-all-start.4) | async-done | bytes 1179680 | tf_op jit(solution)/shard_map/all_to_all | solution.py:90
  739.3 2.5 all_to_all.62
  741.8 4.0 gather_fusion.3
  745.8 1.3 bitcast_reduce_fusion
  (27 shorter events, 0.1 us)
Async XLA Ops:
  7.2 544.6 %copy-start = (bf16[1,192,2048]{2,1,0:T(8,128)(2,1)S(1)}, bf16[1,192,2048]{2,1,0:T(8,128)(2,1)}, u32[]{:S(2)}) copy-start(bf16[1,192,2048]{2,1,0:T(8,128)(2,1)} %param.13) | copy-start | bytes 2359300
  9.0 10.6 %copy-start.6 = (bf16[128,512]{1,0:T(8,128)(2,1)S(1)}, bf16[128,512]{1,0:T(8,128)(2,1)}, u32[]{:S(2)}) copy-start(bf16[128,512]{1,0:T(8,128)(2,1)} %param.7) | copy-start | bytes 393220
  51.9 21.3 %copy-start.7 = (bf16[128,512]{1,0:T(8,128)(2,1)S(1)}, bf16[128,512]{1,0:T(8,128)(2,1)}, u32[]{:S(2)}) copy-start(bf16[128,512]{1,0:T(8,128)(2,1)} %param.8) | copy-start | bytes 393220
  51.9 232.2 %all-to-all-start.1 = ((bf16[128,9,2048]{2,1,0:T(8,128)(2,1)}), bf16[128,9,2048]{2,1,0:T(8,128)(2,1)}, u32[]{:S(2)}, u32[]{:S(2)}) async-start(bf16[128,9,2048]{2,1,0:T(8,128)(2,1)} %broadcast_multiply_fusion), calls=%async_computation.1 | async-start | bytes 16777216 | tf_op jit(solution)/shard_map/all_to_all | solution.py:54
  284.1 259.1 %all-to-all-start = ((bf16[128,9,2048]{2,1,0:T(8,128)(2,1)}), bf16[128,9,2048]{2,1,0:T(8,128)(2,1)}, u32[]{:S(2)}, u32[]{:S(2)}) async-start(bf16[128,9,2048]{2,1,0:T(8,128)(2,1)} %multiply_convert_fusion), calls=%async_computation | async-start | bytes 16777216 | tf_op jit(solution)/shard_map/all_to_all | solution.py:55
  332.1 8.7 %copy-start.3 = (bf16[1,192,2048]{2,1,0:T(8,128)(2,1)S(1)}, bf16[1,192,2048]{2,1,0:T(8,128)(2,1)}, u32[]{:S(2)}) copy-start(bf16[1,192,2048]{2,1,0:T(8,128)(2,1)} %param.12) | copy-start | bytes 2359300
  332.2 293.2 %all-gather.3.cloned.1.call-start = ((), (), s32[]{:S(2)}) async-start(), calls=%async_computation.5 | async-start | bytes 2211840 | tf_op jit(solution)/shard_map/all_gather | solution.py:80
  340.8 5.1 copy-start.1
  340.8 5.1 copy-start.2
  557.3 111.1 %all-gather.5.cloned.1.call-start = ((), (), s32[]{:S(2)}) async-start(), calls=%async_computation.6 | async-start | bytes 2211840 | tf_op jit(solution)/shard_map/all_gather | solution.py:85
  559.6 12.3 %all-to-all-start.2 = ((bf16[192,4,512]{2,0,1:T(8,128)(2,1)}), bf16[192,4,512]{2,0,1:T(8,128)(2,1)S(1)}, u32[]{:S(2)}, u32[]{:S(2)}) async-start(bf16[192,4,512]{2,0,1:T(8,128)(2,1)} %copy.22), calls=%async_computation.2 | async-start | bytes 1572864 | tf_op jit(solution)/shard_map/all_to_all | solution.py:76
  572.0 57.4 %all-to-all-start.3 = ((bf16[192,4,512]{2,0,1:T(8,128)(2,1)}), bf16[192,4,512]{2,0,1:T(8,128)(2,1)S(1)}, u32[]{:S(2)}, u32[]{:S(2)}) async-start(bf16[192,4,512]{2,0,1:T(8,128)(2,1)} %copy.23), calls=%async_computation.3 | async-start | bytes 1572864 | tf_op jit(solution)/shard_map/all_to_all | solution.py:77
  671.7 16.7 %copy-start.5 = (bf16[1152,192]{0,1:T(8,128)(2,1)S(1)}, bf16[1152,192]{0,1:T(8,128)(2,1)}, u32[]{:S(2)}) copy-start(bf16[1152,192]{0,1:T(8,128)(2,1)} %get-tuple-element.6) | copy-start | bytes 1327108
  673.3 19.7 %copy-start.4 = (bf16[1152,192]{0,1:T(8,128)(2,1)S(1)}, bf16[1152,192]{0,1:T(8,128)(2,1)}, u32[]{:S(2)}) copy-start(bf16[1152,192]{0,1:T(8,128)(2,1)} %get-tuple-element.7) | copy-start | bytes 1327108
  673.3 66.0 %all-to-all-start.4 = ((bf16[128,9,512]{2,1,0:T(8,128)(2,1)}), bf16[128,9,512]{2,1,0:T(8,128)(2,1)}, u32[]{:S(2)}, u32[]{:S(2)}) async-start(bf16[128,9,512]{2,1,0:T(8,128)(2,1)} %all_to_all.60), calls=%async_computation.4 | async-start | bytes 4194304 | tf_op jit(solution)/shard_map/all_to_all | solution.py:90
  688.4 9.0 %slice-start = ((s8[4718592]{0:T(1024)(128)(4,1)}), s8[4194304]{0:T(1024)(128)(4,1)S(1)}, s32[]{:S(2)}) async-start(s8[4718592]{0:T(1024)(128)(4,1)} %bitcast.48), calls=%async_computation.7 | async-start | bytes 8388608
  688.4 9.0 %slice-start.1 = ((s8[4718592]{0:T(1024)(128)(4,1)}), s8[524288]{0:T(1024)(128)(4,1)S(1)}, s32[]{:S(2)}) async-start(s8[4718592]{0:T(1024)(128)(4,1)} %bitcast.48), calls=%async_computation.8 | async-start | bytes 1048576
  688.4 9.0 %copy-start.8 = (f32[1152,192]{0,1:T(8,128)S(1)}, f32[1152,192]{0,1:T(8,128)}, u32[]{:S(2)}) copy-start(f32[1152,192]{0,1:T(8,128)} %fusion.10) | copy-start | bytes 2654212
  688.4 9.0 %copy-start.9 = (f32[1152,192]{0,1:T(8,128)S(1)}, f32[1152,192]{0,1:T(8,128)}, u32[]{:S(2)}) copy-start(f32[1152,192]{0,1:T(8,128)} %fusion.8) | copy-start | bytes 2654212
Sparse Core Ops, SparseCore 0:
  557.4 67.8 all-gather.2
  628.0 40.3 all-gather.4
where the time goes:
time: 757 us; the launch traced here: 754 us
  waiting for transfers between devices  505 us (67%)
  starting transfers between devices  91.9 us (12%)
  local copies, waits for them, and re-layouts  69 us (9%)
  matrix products  32 us (4%)
  blocking collectives  23 us (3%)
  other arithmetic  18.5 us (2%)
  between operations  14.3 us (2%)
    all_to_all x1, waiting for transfers between devices, body(): lax.all_to_all(grads_sent, 'expert', split_axis=0, concat_axis=0, tiled=T...  195 us
    all_to_all x1, waiting for transfers between devices, body(): lax.all_to_all(inputs_sent, 'expert', split_axis=0, concat_axis=0, tiled=...  175 us
    all_gather x1, waiting for transfers between devices, body(): lax.all_gather(gate_term, 'etp', axis=1, tiled=True)  49.8 us
    all_to_all x1, starting transfers between devices, body(): lax.all_to_all(grads_sent, 'expert', split_axis=0, concat_axis=0, tiled=T...  48 us
    all_to_all x1, waiting for transfers between devices, body(): lax.all_to_all(slot_grads, 'expert', split_axis=0, concat_axis=0, tiled=T...  39.7 us
    all_gather x1, waiting for transfers between devices, body(): lax.all_gather(up_term, 'etp', axis=1, tiled=True)  39.1 us
    all_to_all x1, starting transfers between devices, body(): lax.all_to_all(inputs_sent, 'expert', split_axis=0, concat_axis=0, tiled=...  21.1 us
  transfers between devices with their start and end apart: 7, of which 6 were waited for; matrix products, arithmetic and copies ran while one was open for 7% of the time, Pallas kernels for 0%

commit v1 on v0

v1 whole, which is shorter than its diff:
```python
import functools

import jax
import jax.numpy as jnp
from jax import lax
from jax.experimental import pallas as pl
from jax.experimental.pallas import tpu as pltpu
from jax.sharding import PartitionSpec as P

MESH = pl.DeviceIdType.MESH
BF16 = jnp.bfloat16
F32 = jnp.float32
LANES = 128
MAIN = 8
STRIDE = 37
CHUNKS = 8


def dot(a, b, dims=(((1,), (0,)), ((), ()))):
    return lax.dot_general(a, b, dims, preferred_element_type=F32)


LAST = (((1,), (1,)), ((), ()))
FIRST = (((0,), (0,)), ((), ()))


def kernel(
    n_e, n_x, nq,
    tokens, grads, routes, combine, wg_h, wu_h, wd_h,
    o_tok, o_gate, o_up, o_down,
    wg, wu, wd, wsw, place_t, weight_t, pt, pot, ovf, send, gath, ovs, xs, gs,
    acts, terms, back, ret,
    w_sem, ws_s, ws_r, a_s, a_r, g1_s, g1_r, g2_s, g2_r, t1_s, t1_r, t2_s, t2_r, b_s, b_r,
):
    tok, feat = tokens.shape
    top = routes.shape[1]
    nc = feat // LANES
    hid = wg.shape[0]
    ns = n_e // nq
    rows = ns * (MAIN + 1)
    half = ns // 2
    cut = (rows // 2 + 15) // 16 * 16
    me = lax.axis_index("expert")
    xi = lax.axis_index("etp")
    right = lax.rem(xi + 1, n_x)
    left = lax.rem(xi + n_x - 1, n_x)

    def remote(src, dst, s, r, dev):
        return pltpu.make_async_remote_copy(
            src_ref=src, dst_ref=dst, send_sem=s, recv_sem=r, device_id=dev, device_id_type=MESH
        )

    def drain(ref, sem):
        pltpu.make_async_copy(ref, ref, sem).wait()

    bar = pltpu.get_barrier_semaphore()

    def greet(off, carry):
        pl.semaphore_signal(
            bar, inc=1, device_id={"expert": lax.rem(me + off, n_e)}, device_id_type=MESH
        )
        return carry

    lax.fori_loop(1, n_e, greet, 0)
    for d in range(1, n_x):
        pl.semaphore_signal(
            bar, inc=1, device_id={"etp": lax.rem(xi + d, n_x)}, device_id_type=MESH
        )

    loads = [
        pltpu.make_async_copy(src, dst, w_sem.at[n])
        for n, (src, dst) in enumerate(((wg_h, wg), (wu_h, wu), (wd_h, wd)))
    ]
    for load in loads:
        load.start()

    chosen = routes[...]
    share = combine[...]
    label = lax.broadcasted_iota(jnp.int32, (tok, n_e), 1)
    hit = jnp.zeros((tok, n_e), F32)
    weight = jnp.zeros((tok, n_e), F32)
    for k in range(top):
        same = chosen[:, k : k + 1] == label
        hit = hit + jnp.where(same, 1.0, 0.0)
        weight = weight + jnp.where(same, share[:, k : k + 1], 0.0)
    lower = (
        lax.broadcasted_iota(jnp.int32, (tok, tok), 0)
        > lax.broadcasted_iota(jnp.int32, (tok, tok), 1)
    )
    lower = jnp.where(lower, 1.0, 0.0).astype(BF16)
    place = jnp.where(hit > 0.5, dot(lower, hit.astype(BF16)), -1.0)
    place_t[...] = place.T
    weight_t[...] = weight.T

    slot_id = lax.broadcasted_iota(jnp.int32, (MAIN, tok), 0).astype(F32)

    def pack(b, carry):
        base = b * ns
        hits, scales = [], []
        for u in range(ns):
            row = jnp.broadcast_to(place_t[pl.ds(base + u, 1), :], (MAIN, tok))
            wrow = jnp.broadcast_to(weight_t[pl.ds(base + u, 1), :], (MAIN, tok))
            same = row == slot_id
            hits.append(jnp.where(same, 1.0, 0.0))
            scales.append(jnp.sum(jnp.where(same, wrow, 0.0), axis=1, keepdims=True))
        pick = jnp.concatenate(hits, axis=0)
        scale = jnp.concatenate(scales, axis=0)
        pt[b] = pick.T.astype(BF16)
        pick = pick.astype(BF16)
        x = dot(pick, tokens[...])
        g = dot(pick, grads[...]) * scale
        for c in range(nc):
            cols = slice(c * LANES, (c + 1) * LANES)
            send[pl.ds(base, ns), c] = x[:, cols].reshape(ns, MAIN, LANES).astype(BF16)
            send[pl.ds(base, ns), nc + c] = g[:, cols].reshape(ns, MAIN, LANES).astype(BF16)
        return carry

    lax.fori_loop(0, nq, pack, 0)
    same = place_t[...] == float(MAIN)
    scale = jnp.sum(jnp.where(same, weight_t[...], 0.0), axis=1, keepdims=True)
    pick = jnp.where(same, 1.0, 0.0)
    pot[...] = pick.T.astype(BF16)
    pick = pick.astype(BF16)
    x = dot(pick, tokens[...])
    g = dot(pick, grads[...]) * scale
    for c in range(nc):
        cols = slice(c * LANES, (c + 1) * LANES)
        ovf[:, c, :] = x[:, cols]
        ovf[:, nc + c, :] = g[:, cols]
    send[:, 2 * nc] = ovf[...].astype(BF16)

    pl.semaphore_wait(bar, n_e - 1 + n_x - 1)

    def swap(n, src, d):
        j = lax.rem(xi + d, n_x)
        cols = pl.ds(pl.multiple_of(j * feat, LANES), feat)
        return remote(
            src.at[:, cols], wsw.at[xi, pl.ds(n * hid, hid)],
            ws_s.at[n, d], ws_r.at[n, d], {"etp": j},
        )

    own_cols = pl.ds(pl.multiple_of(xi * feat, LANES), feat)
    own_swap = [
        pltpu.make_async_copy(src.at[:, own_cols], wsw.at[xi, pl.ds(n * hid, hid)], ws_r.at[n, 0])
        for n, src in enumerate((wg_h, wu_h))
    ]
    for n, src in enumerate((wg_h, wu_h)):
        own_swap[n].start()
        for d in range(1, n_x):
            swap(n, src, d).start()

    own = pltpu.make_async_copy(send.at[me], gath.at[xi, 0], a_r.at[0])
    own.start()

    def dispatch(k, carry):
        dest = lax.rem(me + lax.rem(k * STRIDE, n_e), n_e)
        q = k // ns
        remote(send.at[dest], gath.at[xi, k], a_s.at[q], a_r.at[q], {"expert": dest}).start()
        return carry

    lax.fori_loop(1, n_e, dispatch, 0)

    for load in loads:
        load.wait()

    def to_right(ref, s, r, n, q):
        return remote(ref, ref, s.at[n, q], r.at[n, q], {"etp": right})

    def to_left(ref, s, r, n, q):
        return remote(ref, ref, s.at[n, q], r.at[n, q], {"etp": left})

    def stage1(q):
        mine = gath.at[xi, pl.ds(q * ns, ns)]
        drain(mine, a_r.at[q])
        to_right(mine, g1_s, g1_r, 0, q).start()
        to_left(mine, g1_s, g1_r, 1, q).start()

    def stage2(q):
        drain(gath.at[left, pl.ds(q * ns, ns)], g1_r.at[0, q])
        to_right(gath.at[left, pl.ds(q * ns, half)], g2_s, g2_r, 0, q).start()
        drain(gath.at[right, pl.ds(q * ns, ns)], g1_r.at[1, q])
        to_left(gath.at[right, pl.ds(q * ns + half, ns - half)], g2_s, g2_r, 1, q).start()

    def stage3(q):
        far = lax.rem(xi + 2, n_x)
        base = q * ns
        drain(gath.at[far, pl.ds(base, half)], g2_r.at[0, q])
        drain(gath.at[far, pl.ds(base + half, ns - half)], g2_r.at[1, q])
        at = pl.multiple_of(q * rows, 16)
        over = pl.multiple_of(q * rows + ns * MAIN, 16)
        for j in range(n_x):
            ovs[...] = gath[j, pl.ds(base, ns), 2 * nc].astype(F32)
            for c in range(nc):
                cols = slice(j * feat + c * LANES, j * feat + (c + 1) * LANES)
                x = gath[j, pl.ds(base, ns), c]
                g = gath[j, pl.ds(base, ns), nc + c]
                xs[pl.ds(at, ns * MAIN), cols] = x.reshape(ns * MAIN, LANES)
                gs[pl.ds(at, ns * MAIN), cols] = g.reshape(ns * MAIN, LANES)
                xs[pl.ds(over, ns), cols] = ovs[:, c, :].astype(BF16)
                gs[pl.ds(over, ns), cols] = ovs[:, nc + c, :].astype(BF16)
        x = xs[pl.ds(at, rows), :]
        gate = dot(x, wg[...], LAST)
        up = dot(x, wu[...], LAST)
        hidden = dot(gs[pl.ds(at, rows), :], wd[...], LAST)
        sigma = jax.nn.sigmoid(gate)
        silu = gate * sigma
        acts[pl.ds(at, rows), :] = (silu * up).astype(BF16)
        gate_term = hidden * up * sigma * (1.0 + gate * (1.0 - sigma))
        up_term = hidden * silu
        both = jnp.concatenate([gate_term, up_term], axis=1)
        terms[xi, pl.ds(at, rows), :] = both.astype(BF16)
        mine = terms.at[xi, pl.ds(at, rows)]
        to_right(mine, t1_s, t1_r, 0, q).start()
        to_left(mine, t1_s, t1_r, 1, q).start()

    def stage4(q):
        at = pl.multiple_of(q * rows, 16)
        later = pl.multiple_of(q * rows + cut, 16)
        drain(terms.at[left, pl.ds(at, rows)], t1_r.at[0, q])
        to_right(terms.at[left, pl.ds(at, cut)], t2_s, t2_r, 0, q).start()
        drain(terms.at[right, pl.ds(at, rows)], t1_r.at[1, q])
        to_left(terms.at[right, pl.ds(later, rows - cut)], t2_s, t2_r, 1, q).start()

    def stage5(q):
        far = lax.rem(xi + 2, n_x)
        base = q * ns
        at = pl.multiple_of(q * rows, 16)
        later = pl.multiple_of(q * rows + cut, 16)
        drain(terms.at[far, pl.ds(at, cut)], t2_r.at[0, q])
        drain(terms.at[far, pl.ds(later, rows - cut)], t2_r.at[1, q])
        slot = dot(terms[0, pl.ds(at, rows), :], wsw[0])
        for j in range(1, n_x):
            slot = slot + dot(terms[j, pl.ds(at, rows), :], wsw[j])
        ovs[...] = jnp.zeros_like(ovs)
        for c in range(nc):
            cols = slice(c * LANES, (c + 1) * LANES)
            main = slot[: ns * MAIN, cols].reshape(ns, MAIN, LANES)
            back[pl.ds(base, ns), c] = main.astype(BF16)
            ovs[:, c, :] = slot[ns * MAIN :, cols]
        back[pl.ds(base, ns), nc] = ovs[...].astype(BF16)

        @pl.when(q == 0)
        def _():
            pltpu.make_async_copy(back.at[0], ret.at[me], b_r).start()

        def answer(k, carry):
            dest = lax.rem(me + n_e - lax.rem(k * STRIDE, n_e), n_e)
            remote(back.at[k], ret.at[me], b_s, b_r, {"expert": dest}).start()
            return carry

        lax.fori_loop(jnp.maximum(base, 1), base + ns, answer, 0)

    def step(t, carry):
        for lag, stage in enumerate((stage1, stage2, stage3, stage4, stage5)):
            q = t - lag
            if stage is stage5:

                @pl.when(q == 0)
                def _():
                    for n, src in enumerate((wg_h, wu_h)):
                        own_swap[n].wait()
                        for d in range(1, n_x):
                            swap(n, src, d).wait_recv()

            @pl.when(jnp.logical_and(q >= 0, q < nq))
            def _():
                stage(q)

        return carry

    lax.fori_loop(0, nq + 4, step, 0)

    mine = terms[xi]
    width = 2 * LANES
    for n in range(feat * n_x // width):
        cols = slice(n * width, (n + 1) * width)
        both = dot(mine, xs[:, cols], FIRST)
        o_gate[:, cols] = both[:hid].astype(BF16)
        o_up[:, cols] = both[hid:].astype(BF16)
        o_down[:, cols] = dot(acts[...], gs[:, cols], FIRST).astype(BF16)

    drain(ret, b_r)
    ovf[...] = ret[:, nc].astype(F32)
    for c in range(nc):
        total = dot(pot[...], ovf[:, c, :].astype(BF16))
        for b in range(nq):
            part = ret[pl.ds(b * ns, ns), c].reshape(ns * MAIN, LANES)
            total = total + dot(pt[b], part)
        o_tok[:, c * LANES : (c + 1) * LANES] = total.astype(BF16)

    for n, src in enumerate((wg_h, wu_h)):
        for d in range(1, n_x):
            swap(n, src, d).wait_send()
    drain(back.at[pl.ds(1, n_e - 1)], b_s)

    def flush(q, carry):
        at = pl.multiple_of(q * rows, 16)
        for n in range(2):
            drain(gath.at[0, pl.ds(q * ns, ns)], g1_s.at[n, q])
            drain(gath.at[0, pl.ds(q * ns, half)], g2_s.at[n, q])
            drain(terms.at[0, pl.ds(at, rows)], t1_s.at[n, q])
            drain(terms.at[0, pl.ds(at, cut if n == 0 else rows - cut)], t2_s.at[n, q])
        return carry

    lax.fori_loop(0, nq, flush, 0)
    drain(send.at[pl.ds(0, ns - 1)], a_s.at[0])

    def flush_a(q, carry):
        drain(send.at[pl.ds(0, ns)], a_s.at[q])
        return carry

    lax.fori_loop(1, nq, flush_a, 0)


def body(tokens, out_grad, routes, combine, w_gate, w_up, w_down):
    n_e = lax.axis_size("expert")
    n_x = lax.axis_size("etp")
    tok, feat = tokens.shape
    hid, width = w_gate.shape[1:]
    nq = min(CHUNKS, n_e // 2)
    ns = n_e // nq
    slots = n_e * (MAIN + 1)
    nc = feat // LANES
    vmem = pl.BlockSpec(memory_space=pltpu.VMEM)
    hbm = pl.BlockSpec(memory_space=pl.ANY)
    dma = pltpu.SemaphoreType.DMA
    grad_shape = jax.ShapeDtypeStruct((hid, width), BF16)
    outs = pl.pallas_call(
        functools.partial(kernel, n_e, n_x, nq),
        out_shape=(jax.ShapeDtypeStruct((tok, feat), BF16), grad_shape, grad_shape, grad_shape),
        in_specs=[vmem] * 4 + [hbm] * 3,
        out_specs=(vmem,) * 4,
        scratch_shapes=[
            pltpu.VMEM((hid, width), BF16),
            pltpu.VMEM((hid, width), BF16),
            pltpu.VMEM((hid, width), BF16),
            pltpu.VMEM((n_x, 2 * hid, feat), BF16),
            pltpu.VMEM((n_e, tok), F32),
            pltpu.VMEM((n_e, tok), F32),
            pltpu.VMEM((nq, tok, ns * MAIN), BF16),
            pltpu.VMEM((tok, n_e), BF16),
            pltpu.VMEM((n_e, MAIN, LANES), F32),
            pltpu.VMEM((n_e, 2 * nc + 1, MAIN, LANES), BF16),
            pltpu.VMEM((n_x, n_e, 2 * nc + 1, MAIN, LANES), BF16),
            pltpu.VMEM((ns, MAIN, LANES), F32),
            pltpu.VMEM((slots, width), BF16),
            pltpu.VMEM((slots, width), BF16),
            pltpu.VMEM((slots, hid), BF16),
            pltpu.VMEM((n_x, slots, 2 * hid), BF16),
            pltpu.VMEM((n_e, nc + 1, MAIN, LANES), BF16),
            pltpu.VMEM((n_e, nc + 1, MAIN, LANES), BF16),
            dma((3,)),
            dma((2, n_x)),
            dma((2, n_x)),
            dma((nq,)),
            dma((nq,)),
        ]
        + [dma((2, nq))] * 8
        + [dma(()), dma(())],
        compiler_params=pltpu.CompilerParams(
            collective_id=0, has_side_effects=True, vmem_limit_bytes=62 * 1024 * 1024
        ),
    )(tokens, out_grad, routes, combine, w_gate[0], w_up[0], w_down[0])
    grad_tokens, grad_gate, grad_up, grad_down = outs
    return grad_tokens, grad_gate[None], grad_up[None], grad_down[None]


def solution(mesh):
    placed = (
        P("expert", "etp"),
        P("expert", "etp"),
        P("expert", None),
        P("expert", None),
        P("expert", "etp", None),
        P("expert", "etp", None),
        P("expert", "etp", None),
    )
    return jax.shard_map(
        body,
        mesh=mesh,
        in_specs=placed,
        out_specs=(
            P("expert", "etp"),
            P("expert", "etp", None),
            P("expert", "etp", None),
            P("expert", "etp", None),
        ),
        check_vma=False,
    )
```

time: 757 us -> 167 us (0.22)
  waiting for transfers between devices: 505 us -> 0 us
  Pallas kernels: 0 us -> 158 us
  starting transfers between devices: 91.9 us -> 0 us
  local copies, waits for them, and re-layouts: 69 us -> 8.17 us
  matrix products: 32 us -> 0 us
  blocking collectives: 23 us -> 0 us
  other arithmetic: 18.5 us -> 0 us
  between operations: 14.3 us -> 0.65 us
    all_to_all x5 -> x0, waiting for transfers between devices: 416 us -> none  [the longest x1 195 us: body(): lax.all_to_all(grads_sent, 'expert', split_axis=0, concat_axis=0, tiled=T...]
    pallas_call x0 -> x1, Pallas kernels: none -> 158 us  [body(): pl.pallas_call(functools.partial(kernel, n_e, n_x, nq), out_shape=(jax.Sh...]
    all_to_all x5 -> x0, starting transfers between devices: 91.6 us -> none  [the longest x1 48 us: body(): lax.all_to_all(grads_sent, 'expert', split_axis=0, concat_axis=0, tiled=T...]
    all_gather x2 -> x0, waiting for transfers between devices: 88.9 us -> none  [the longest x1 49.8 us: body(): lax.all_gather(gate_term, 'etp', axis=1, tiled=True)]
    dot_general x9 -> x0, matrix products: 32 us -> none  [the longest x1 5.55 us: body(): lax.dot_general(rows_g, down_w, contract_last, preferred_element_type=jnp...]
    gather x5 -> x0, local copies, waits for them, and re-layouts: 28.6 us -> none  [the longest x2 14 us: pack_rows(): inputs_sent = token_rows[token_of] * mask]
    all_to_all x8 -> x0, local copies, waits for them, and re-layouts: 24.2 us -> none  [the longest x1 8.5 us: body(): lax.all_to_all(grads_sent, 'expert', split_axis=0, concat_axis=0, tiled=T...]
    all_gather x2 -> x0, blocking collectives: 23 us -> none  [the longest x1 11.9 us: body(): lax.all_gather(out_grad, 'etp', axis=1, tiled=True)]
  transfers between devices with their start and end apart: 7 -> 0, of which waited for: 6 -> 0; matrix products, arithmetic and copies ran while one was open for 7% -> 0% of each run, Pallas kernels for 0% -> 0%
where the time goes in v1:
time: 167 us
  Pallas kernels  158 us (95%)
  local copies, waits for them, and re-layouts  8.17 us (5%)
    pallas_call x1, Pallas kernels, body(): pl.pallas_call(functools.partial(kernel, n_e, n_x, nq), out_shape=(jax.Sh...  158 us
    unnamed x14, local copies, waits for them, and re-layouts  8.17 us

profile of v1, /device:TPU:1, one launch (start us, length us, event | category | flops | bytes accessed | tf_op | source)
XLA Modules:
  0.0 166.8 jit_solution(3662047060952729859)
XLA Ops:
  0.6 0.0 copy-start.2
  0.6 0.7 copy-done.2
  1.3 0.0 copy-start.3
  1.3 0.7 copy.11.routes
  2.0 0.0 copy-done.3
  2.1 0.7 copy.12.combine
  2.8 158.0 %shard_map.102 = (bf16[128,512]{1,0:T(8,128)(2,1)}, bf16[192,2048]{1,0:T(8,128)(2,1)}, bf16[192,2048]{1,0:T(8,128)(2,1)}, bf16[192,2048]{1,0:T(8,128)(2,1)}) custom-call(bf16[128,512]{1,0:T(8,128)(2,1)} %tokens.1, bf16[128,512]{1,0:T(8,128)(2,1)} %grads.1, s32[128,8]{1,0:T(8,128)} %copy.11.routes, f32[128,8]{1,0:T(8,128)} %copy.12.combine, ...), custom_call_target="tpu_custom_call" | custom-call | tf_op jit(solution)/shard_map/pallas_call | solution.py:328
  160.8 1.6 copy.17
  162.4 0.0 copy-start.1
  162.4 2.2 %copy.18 = bf16[1,192,2048]{2,1,0:T(8,128)(2,1)} copy(bf16[1,192,2048]{2,1,0:T(8,128)(2,1)} %bitcast.8) | data formatting | bytes 1572864
  164.5 0.0 copy-done.1
  164.5 0.0 copy-start
  164.5 0.9 copy.19
  165.4 0.5 copy-done
  165.9 0.9 copy.20
Async XLA Ops:
  0.6 0.7 copy-start.2
  1.3 0.7 copy-start.3
  162.4 2.2 %copy-start.1 = (bf16[192,2048]{1,0:T(8,128)(2,1)S(1)}, bf16[192,2048]{1,0:T(8,128)(2,1)}, u32[]{:S(2)}) copy-start(bf16[192,2048]{1,0:T(8,128)(2,1)} %get-tuple-element.10) | copy-start | bytes 2359300
  164.5 1.4 copy-start

commit v2 on v1

v2 whole, which is shorter than its diff:
```python
import functools

import jax
import jax.numpy as jnp
from jax import lax
from jax.experimental import pallas as pl
from jax.experimental.pallas import tpu as pltpu
from jax.sharding import PartitionSpec as P

MESH = pl.DeviceIdType.MESH
BF16 = jnp.bfloat16
F32 = jnp.float32
LANES = 128
MAIN = 8
STRIDE = 37
CHUNKS = 8
VMEM_MIB = 48


def dot(a, b, dims=(((1,), (0,)), ((), ()))):
    return lax.dot_general(a, b, dims, preferred_element_type=F32)


LAST = (((1,), (1,)), ((), ()))
FIRST = (((0,), (0,)), ((), ()))


def kernel(
    n_e, n_x, nq,
    tokens, grads, routes, combine, wg_h, wu_h, wd_h,
    o_tok, o_gate, o_up, o_down,
    wt, place_t, weight_t, pt, pot, ovf, send, ga, gp, ovs, xs, gs,
    gu_own, h_own, ps, pr, tm, tp, y_own, ys, yr, back, ret, acc, dwo, dwp,
    wl_sem, w_s, w_r, a_s, a_r, g_s, g_r, p_s, p_r, t_s, t_r, y_s, y_r, b_s, b_r, d_s, d_r, o_sem,
):
    tok, feat = tokens.shape
    top = routes.shape[0]
    nc = feat // LANES
    hid = wg_h.shape[0]
    gu = 2 * hid
    wide = ps.shape[1]
    ns = n_e // nq
    rows = ns * (MAIN + 1)
    me = lax.axis_index("expert")
    xi = lax.axis_index("etp")
    parity = lax.rem(me, 2)
    turn = lax.rem(xi + parity, n_x)
    xa = lax.rem(turn + 1 - 2 * lax.rem(turn, 2) + n_x - parity, n_x)
    xb = lax.rem(n_x - 1 - turn + n_x - parity, n_x)
    xd = lax.rem(n_x - 1 - turn + 1 - 2 * lax.rem(n_x - 1 - turn, 2) + n_x - parity, n_x)
    on_a, on_b = {"etp": xa}, {"etp": xb}

    def remote(src, dst, s, r, dev):
        return pltpu.make_async_remote_copy(
            src_ref=src, dst_ref=dst, send_sem=s, recv_sem=r, device_id=dev, device_id_type=MESH
        )

    def drain(ref, sem):
        pltpu.make_async_copy(ref, ref, sem).wait()

    def cols_of(x):
        return pl.ds(pl.multiple_of(x * feat, LANES), feat)

    bar = pltpu.get_barrier_semaphore()
    for dev in (on_a, on_b):
        pl.semaphore_signal(bar, inc=1, device_id=dev, device_id_type=MESH)

    def greet(off, carry):
        pl.semaphore_signal(
            bar, inc=1, device_id={"expert": lax.rem(me + off, n_e)}, device_id_type=MESH
        )
        return carry

    lax.fori_loop(1, n_e, greet, 0)

    weights = (wg_h, wu_h, wd_h)
    loads = [
        pltpu.make_async_copy(
            src.at[:, cols_of(x)],
            wt.at[0, pl.ds(n * hid, hid), pl.ds(h * feat, feat)],
            wl_sem.at[n, h],
        )
        for n, src in enumerate(weights)
        for h, x in enumerate((xi, xa))
    ]
    for load in loads:
        load.start()

    label = lax.broadcasted_iota(jnp.int32, (n_e, tok), 0)
    hit = jnp.zeros((n_e, tok), F32)
    weight = jnp.zeros((n_e, tok), F32)
    for k in range(top):
        same = routes[k : k + 1, :] == label
        hit = hit + jnp.where(same, 1.0, 0.0)
        weight = weight + jnp.where(same, combine[k : k + 1, :], 0.0)
    earlier = (
        lax.broadcasted_iota(jnp.int32, (tok, tok), 0)
        < lax.broadcasted_iota(jnp.int32, (tok, tok), 1)
    )
    earlier = jnp.where(earlier, 1.0, 0.0).astype(BF16)
    place_t[...] = jnp.where(hit > 0.5, dot(hit.astype(BF16), earlier), -1.0)
    weight_t[...] = weight

    pl.semaphore_wait(bar, n_e - 1 + 2)

    swaps = [
        remote(
            src.at[:, cols_of(x)],
            wt.at[1, pl.ds(n * hid, hid), pl.ds(h * feat, feat)],
            w_s.at[n, h], w_r.at[n, h], on_b,
        )
        for n, src in enumerate(weights)
        for h, x in enumerate((xb, xd))
    ]
    for swap in swaps:
        swap.start()

    slot_id = lax.broadcasted_iota(jnp.int32, (MAIN, tok), 0).astype(F32)

    def pack(b, carry):
        base = b * ns
        hits, scales = [], []
        for u in range(ns):
            row = jnp.broadcast_to(place_t[pl.ds(base + u, 1), :], (MAIN, tok))
            wrow = jnp.broadcast_to(weight_t[pl.ds(base + u, 1), :], (MAIN, tok))
            same = row == slot_id
            hits.append(jnp.where(same, 1.0, 0.0))
            scales.append(jnp.sum(jnp.where(same, wrow, 0.0), axis=1, keepdims=True))
        pick = jnp.concatenate(hits, axis=0)
        scale = jnp.concatenate(scales, axis=0)
        pt[b] = pick.T.astype(BF16)
        pick = pick.astype(BF16)
        x = dot(pick, tokens[...])
        g = dot(pick, grads[...]) * scale
        for c in range(nc):
            cols = slice(c * LANES, (c + 1) * LANES)
            send[pl.ds(base, ns), c] = x[:, cols].reshape(ns, MAIN, LANES).astype(BF16)
            send[pl.ds(base, ns), nc + c] = g[:, cols].reshape(ns, MAIN, LANES).astype(BF16)
        return carry

    lax.fori_loop(0, nq, pack, 0)
    same = place_t[...] == float(MAIN)
    scale = jnp.sum(jnp.where(same, weight_t[...], 0.0), axis=1, keepdims=True)
    pick = jnp.where(same, 1.0, 0.0)
    pot[...] = pick.T.astype(BF16)
    pick = pick.astype(BF16)
    x = dot(pick, tokens[...])
    g = dot(pick, grads[...]) * scale
    for c in range(nc):
        cols = slice(c * LANES, (c + 1) * LANES)
        ovf[:, c, :] = x[:, cols]
        ovf[:, nc + c, :] = g[:, cols]
    send[:, 2 * nc] = ovf[...].astype(BF16)

    pltpu.make_async_copy(send.at[me], ga.at[0], a_r.at[0]).start()

    def dispatch(k, carry):
        dest = lax.rem(me + lax.rem(k * STRIDE, n_e), n_e)
        q = k // ns
        remote(send.at[dest], ga.at[k], a_s.at[q], a_r.at[q], {"expert": dest}).start()
        return carry

    lax.fori_loop(1, n_e, dispatch, 0)

    def at(q):
        return pl.ds(pl.multiple_of(q * rows, 16), rows)

    def stage1(q):
        mine = pl.ds(q * ns, ns)
        drain(ga.at[mine], a_r.at[q])
        remote(ga.at[mine], gp.at[mine], g_s.at[q], g_r.at[q], on_a).start()

    def stage2(q):
        base = q * ns
        drain(gp.at[pl.ds(base, ns)], g_r.at[q])
        main = pl.ds(pl.multiple_of(q * rows, 16), ns * MAIN)
        over = pl.ds(pl.multiple_of(q * rows + ns * MAIN, 16), ns)
        for j, buf in enumerate((ga, gp)):
            ovs[...] = buf[pl.ds(base, ns), 2 * nc].astype(F32)
            for c in range(nc):
                cols = slice(j * feat + c * LANES, j * feat + (c + 1) * LANES)
                xs[main, cols] = buf[pl.ds(base, ns), c].reshape(ns * MAIN, LANES)
                gs[main, cols] = buf[pl.ds(base, ns), nc + c].reshape(ns * MAIN, LANES)
                xs[over, cols] = ovs[:, c, :].astype(BF16)
                gs[over, cols] = ovs[:, nc + c, :].astype(BF16)
        x = xs[at(q), :]
        g = gs[at(q), :]
        ps[at(q), :gu] = dot(x, wt[1, :gu], LAST).astype(BF16)
        part = dot(g, wt[1, gu:], LAST)
        pad = jnp.zeros((rows, wide - gu - hid), F32)
        ps[at(q), gu:] = jnp.concatenate([part, pad], axis=1).astype(BF16)
        remote(ps.at[at(q)], pr.at[at(q)], p_s.at[q], p_r.at[q], on_b).start()
        gu_own[at(q), :] = dot(x, wt[0, :gu], LAST)
        h_own[at(q), :] = dot(g, wt[0, gu:], LAST)

    def stage3(q):
        drain(pr.at[at(q)], p_r.at[q])
        both = gu_own[at(q), :] + pr[at(q), :gu].astype(F32)
        hidden = h_own[at(q), :] + pr[at(q), gu : gu + hid].astype(F32)
        gate = both[:, :hid]
        up = both[:, hid:]
        sigma = jax.nn.sigmoid(gate)
        silu = gate * sigma
        gate_term = hidden * up * sigma * (1.0 + gate * (1.0 - sigma))
        up_term = hidden * silu
        tm[at(q), :gu] = jnp.concatenate([gate_term, up_term], axis=1).astype(BF16)
        pad = jnp.zeros((rows, wide - gu - hid), F32)
        tm[at(q), gu:] = jnp.concatenate([silu * up, pad], axis=1).astype(BF16)
        remote(tm.at[at(q)], tp.at[at(q)], t_s.at[q], t_r.at[q], on_b).start()

    def stage4(q):
        drain(tp.at[at(q)], t_r.at[q])
        mine = tm[at(q), :gu]
        theirs = tp[at(q), :gu]
        part = dot(mine, wt[0, :gu, feat:]) + dot(theirs, wt[1, :gu, feat:])
        ys[at(q), :] = part.astype(BF16)
        remote(ys.at[at(q)], yr.at[at(q)], y_s.at[q], y_r.at[q], on_a).start()
        y_own[at(q), :] = dot(mine, wt[0, :gu, :feat]) + dot(theirs, wt[1, :gu, :feat])

    def stage5(q):
        base = q * ns
        drain(yr.at[at(q)], y_r.at[q])
        slot = y_own[at(q), :] + yr[at(q), :].astype(F32)
        ovs[...] = jnp.zeros_like(ovs)
        for c in range(nc):
            cols = slice(c * LANES, (c + 1) * LANES)
            main = slot[: ns * MAIN, cols].reshape(ns, MAIN, LANES)
            back[pl.ds(base, ns), c] = main.astype(BF16)
            ovs[:, c, :] = slot[ns * MAIN :, cols]
        back[pl.ds(base, ns), nc] = ovs[...].astype(BF16)

        @pl.when(q == 0)
        def _():
            pltpu.make_async_copy(back.at[0], ret.at[me], b_r).start()

        def answer(k, carry):
            dest = lax.rem(me + n_e - lax.rem(k * STRIDE, n_e), n_e)
            remote(back.at[k], ret.at[me], b_s, b_r, {"expert": dest}).start()
            return carry

        lax.fori_loop(jnp.maximum(base, 1), base + ns, answer, 0)

    last = nq - max(1, nq // 4)
    middle = (last + 1) // 2
    ranges = [(0, middle), (middle, last)] if middle < last else [(0, last)]

    def weight_grads(block, first, stop):
        r = slice(first * rows, stop * rows)
        t = (tm, tp)[block]
        return dot(t[r, :gu], xs[r, :], FIRST), dot(t[r, gu : gu + hid], gs[r, :], FIRST)

    def step(t, carry):
        for lag, stage in enumerate((stage1, stage2, stage3, stage4, stage5)):
            q = t - lag
            if stage is stage2:

                @pl.when(q == 0)
                def _():
                    for load in loads:
                        load.wait()
                    for swap in swaps:
                        swap.wait_recv()

            @pl.when(jnp.logical_and(q >= 0, q < nq))
            def _():
                stage(q)

        for n, (first, stop) in enumerate(ranges):

            @pl.when(t - 3 == stop - 1)
            def _():
                for block in range(2):
                    both, down = weight_grads(block, first, stop)
                    if n == 0:
                        acc[block, :gu] = both
                        acc[block, gu:] = down
                    else:
                        acc[block, :gu] += both
                        acc[block, gu:] += down

        return carry

    lax.fori_loop(0, nq + 4, step, 0)

    outs = (o_gate, o_up, o_down)

    def piece(ref, n, h):
        return ref.at[pl.ds(n * hid, hid), pl.ds(h * feat, feat)]

    both, down = weight_grads(1, last, nq)
    dwp[:gu] = (acc[1, :gu] + both).astype(BF16)
    dwp[gu:] = (acc[1, gu:] + down).astype(BF16)
    theirs = [
        remote(
            piece(dwp, n, h), out.at[:, cols_of(x)], d_s.at[n, h], d_r.at[n, h], on_b
        )
        for n, out in enumerate(outs)
        for h, x in enumerate((xi, xa))
    ]
    for copy in theirs:
        copy.start()
    both, down = weight_grads(0, last, nq)
    dwo[:gu] = (acc[0, :gu] + both).astype(BF16)
    dwo[gu:] = (acc[0, gu:] + down).astype(BF16)
    mine = [
        pltpu.make_async_copy(piece(dwo, n, h), out.at[:, cols_of(x)], o_sem.at[n, h])
        for n, out in enumerate(outs)
        for h, x in enumerate((xi, xa))
    ]
    for copy in mine:
        copy.start()

    drain(ret, b_r)
    ovf[...] = ret[:, nc].astype(F32)
    for c in range(nc):
        total = dot(pot[...], ovf[:, c, :].astype(BF16))
        for b in range(nq):
            part = ret[pl.ds(b * ns, ns), c].reshape(ns * MAIN, LANES)
            total = total + dot(pt[b], part)
        o_tok[:, c * LANES : (c + 1) * LANES] = total.astype(BF16)

    for swap in swaps:
        swap.wait_send()
    drain(back.at[pl.ds(1, n_e - 1)], b_s)
    drain(send.at[pl.ds(0, ns - 1)], a_s.at[0])

    def flush_a(q, carry):
        drain(send.at[pl.ds(0, ns)], a_s.at[q])
        return carry

    lax.fori_loop(1, nq, flush_a, 0)

    def flush(q, carry):
        drain(ga.at[pl.ds(q * ns, ns)], g_s.at[q])
        drain(ps.at[at(q)], p_s.at[q])
        drain(tm.at[at(q)], t_s.at[q])
        drain(ys.at[at(q)], y_s.at[q])
        return carry

    lax.fori_loop(0, nq, flush, 0)
    for copy in mine:
        copy.wait()
    for copy in theirs:
        copy.wait_send()
        copy.wait_recv()


def body(tokens, out_grad, routes, combine, w_gate, w_up, w_down):
    n_e = lax.axis_size("expert")
    n_x = lax.axis_size("etp")
    tok, feat = tokens.shape
    hid, width = w_gate.shape[1:]
    nq = min(CHUNKS, n_e // 2)
    ns = n_e // nq
    slots = n_e * (MAIN + 1)
    nc = feat // LANES
    two = 2 * feat
    wide = (3 * hid + LANES - 1) // LANES * LANES
    vmem = pl.BlockSpec(memory_space=pltpu.VMEM)
    hbm = pl.BlockSpec(memory_space=pl.ANY)
    dma = pltpu.SemaphoreType.DMA
    grad_shape = jax.ShapeDtypeStruct((hid, width), BF16)
    outs = pl.pallas_call(
        functools.partial(kernel, n_e, n_x, nq),
        out_shape=(jax.ShapeDtypeStruct((tok, feat), BF16), grad_shape, grad_shape, grad_shape),
        in_specs=[vmem] * 4 + [hbm] * 3,
        out_specs=(vmem, hbm, hbm, hbm),
        scratch_shapes=[
            pltpu.VMEM((2, 3 * hid, two), BF16),
            pltpu.VMEM((n_e, tok), F32),
            pltpu.VMEM((n_e, tok), F32),
            pltpu.VMEM((nq, tok, ns * MAIN), BF16),
            pltpu.VMEM((tok, n_e), BF16),
            pltpu.VMEM((n_e, MAIN, LANES), F32),
            pltpu.VMEM((n_e, 2 * nc + 1, MAIN, LANES), BF16),
            pltpu.VMEM((n_e, 2 * nc + 1, MAIN, LANES), BF16),
            pltpu.VMEM((n_e, 2 * nc + 1, MAIN, LANES), BF16),
            pltpu.VMEM((ns, MAIN, LANES), F32),
            pltpu.VMEM((slots, two), BF16),
            pltpu.VMEM((slots, two), BF16),
            pltpu.VMEM((slots, 2 * hid), F32),
            pltpu.VMEM((slots, hid), F32),
            pltpu.VMEM((slots, wide), BF16),
            pltpu.VMEM((slots, wide), BF16),
            pltpu.VMEM((slots, wide), BF16),
            pltpu.VMEM((slots, wide), BF16),
            pltpu.VMEM((slots, feat), F32),
            pltpu.VMEM((slots, feat), BF16),
            pltpu.VMEM((slots, feat), BF16),
            pltpu.VMEM((n_e, nc + 1, MAIN, LANES), BF16),
            pltpu.VMEM((n_e, nc + 1, MAIN, LANES), BF16),
            pltpu.VMEM((2, 3 * hid, two), F32),
            pltpu.VMEM((3 * hid, two), BF16),
            pltpu.VMEM((3 * hid, two), BF16),
            dma((3, 2)),
            dma((3, 2)),
            dma((3, 2)),
        ]
        + [dma((nq,))] * 10
        + [dma(()), dma(()), dma((3, 2)), dma((3, 2)), dma((3, 2))],
        compiler_params=pltpu.CompilerParams(
            collective_id=0, has_side_effects=True, vmem_limit_bytes=VMEM_MIB * 1024 * 1024
        ),
    )(tokens, out_grad, routes.T, combine.T, w_gate[0], w_up[0], w_down[0])
    grad_tokens, grad_gate, grad_up, grad_down = outs
    return grad_tokens, grad_gate[None], grad_up[None], grad_down[None]


def solution(mesh):
    placed = (
        P("expert", "etp"),
        P("expert", "etp"),
        P("expert", None),
        P("expert", None),
        P("expert", "etp", None),
        P("expert", "etp", None),
        P("expert", "etp", None),
    )
    return jax.shard_map(
        body,
        mesh=mesh,
        in_specs=placed,
        out_specs=(
            P("expert", "etp"),
            P("expert", "etp", None),
            P("expert", "etp", None),
            P("expert", "etp", None),
        ),
        check_vma=False,
    )
```

time: 167 us -> 158 us (0.946)
  the two profiles are of different devices: /device:TPU:1 before, /device:TPU:64 now
where the time goes in v2:
time: 158 us
  Pallas kernels  148 us (94%)
  local copies, waits for them, and re-layouts  9.19 us (6%)
    pallas_call x1, Pallas kernels, body(): pl.pallas_call(functools.partial(kernel, n_e, n_x, nq), out_shape=(jax.Sh...  148 us
    unnamed x18, local copies, waits for them, and re-layouts  9.19 us

profile of v2, /device:TPU:64, one launch (start us, length us, event | category | flops | bytes accessed | tf_op | source)
XLA Modules:
  0.0 157.7 jit_solution(7628385838563569506)
XLA Ops:
  0.6 0.0 copy-start.6
  0.6 0.0 copy-start.5
  0.7 0.7 copy-done.6
  1.3 0.0 copy-done.5
  1.3 0.0 copy-start
  1.3 1.1 copy-done
  2.5 0.0 copy-start.1
  2.5 1.1 copy-done.1
  3.6 0.0 copy-start.2
  3.6 1.1 copy-done.2
  4.7 0.0 copy-start.3
  4.7 0.9 copy-done.3
  5.6 0.0 copy-start.4
  5.6 0.9 copy-done.4
  6.5 147.9 %shard_map.102 = (bf16[128,512]{1,0:T(8,128)(2,1)S(1)}, bf16[192,2048]{1,0:T(8,128)(2,1)S(1)}, bf16[192,2048]{1,0:T(8,128)(2,1)S(1)}, bf16[192,2048]{1,0:T(8,128)(2,1)S(1)}) custom-call(bf16[128,512]{1,0:T(8,128)(2,1)S(1)} %copy-done.3, bf16[128,512]{1,0:T(8,128)(2,1)S(1)} %copy-done.4, s32[8,128]{1,0:T(8,128)S(1)} %bitcast.14, f32[8,128]{1,0:T(8,128)S(1)} %bitcast.15, ...), custom_call_target="tpu_custom_call" | custom-call | tf_op jit(solution)/shard_map/pallas_call | solution.py:363
  154.4 0.7 copy.15
  155.1 0.9 copy.16
  156.0 0.9 copy.17
  156.8 0.9 copy.18
Async XLA Ops:
  0.6 0.7 copy-start.6
  0.6 0.7 copy-start.5
  1.3 1.1 copy-start
  2.5 1.1 copy-start.1
  3.6 1.1 copy-start.2
  4.7 0.9 copy-start.3
  5.6 0.9 copy-start.4

commit v3 on v2

--- a/solution.py
+++ b/solution.py
@@ -13,6 +13,7 @@
 LANES = 128
 MAIN = 8
 STRIDE = 37
+SPAN = 8
 CHUNKS = 8
 VMEM_MIB = 48
 
@@ -27,11 +28,11 @@
 
 def kernel(
     n_e, n_x, nq,
-    tokens, grads, routes, combine, wg_h, wu_h, wd_h,
+    tok_h, grad_h, route_h, comb_h, wg_h, wu_h, wd_h,
     o_tok, o_gate, o_up, o_down,
-    wt, place_t, weight_t, pt, pot, ovf, send, ga, gp, ovs, xs, gs,
+    tokens, grads, routes, combine, wt, place_t, weight_t, pk, wk, pt, pot, ovf, send, ga, gp, ovs, xs, gs,
     gu_own, h_own, ps, pr, tm, tp, y_own, ys, yr, back, ret, acc, dwo, dwp,
-    wl_sem, w_s, w_r, a_s, a_r, g_s, g_r, p_s, p_r, t_s, t_r, y_s, y_r, b_s, b_r, d_s, d_r, o_sem,
+    in_sem, wl_sem, w_s, w_r, a_s, a_r, g_s, g_r, p_s, p_r, t_s, t_r, y_s, y_r, b_s, b_r, d_s, d_r, o_sem,
 ):
     tok, feat = tokens.shape
     top = routes.shape[0]
@@ -61,6 +62,27 @@
     def cols_of(x):
         return pl.ds(pl.multiple_of(x * feat, LANES), feat)
 
+    span = min(SPAN, n_e // 2)
+    layers = n_e // (2 * span)
+
+    def partner(k, ahead):
+        m = lax.rem(k * STRIDE, n_e)
+        step_c, step_y, step_z = lax.rem(m, 2), lax.rem(m // 2, span), m // (2 * span)
+        if not ahead:
+            step_c, step_y, step_z = 2 - step_c, span - step_y, layers - step_z
+        z = lax.rem(me // (2 * span) + step_z, layers)
+        y = lax.rem(lax.rem(me // 2, span) + step_y, span)
+        return (z * span + y) * 2 + lax.rem(lax.rem(me, 2) + step_c, 2)
+
+    reads = [
+        pltpu.make_async_copy(src, dst, in_sem.at[n])
+        for n, (src, dst) in enumerate(
+            ((route_h, routes), (comb_h, combine), (tok_h, tokens), (grad_h, grads))
+        )
+    ]
+    for read in reads:
+        read.start()
+
     bar = pltpu.get_barrier_semaphore()
     for dev in (on_a, on_b):
         pl.semaphore_signal(bar, inc=1, device_id=dev, device_id_type=MESH)
@@ -86,6 +108,8 @@
     for load in loads:
         load.start()
 
+    for read in reads:
+        read.wait()
     label = lax.broadcasted_iota(jnp.int32, (n_e, tok), 0)
     hit = jnp.zeros((n_e, tok), F32)
     weight = jnp.zeros((n_e, tok), F32)
@@ -117,50 +141,54 @@
 
     slot_id = lax.broadcasted_iota(jnp.int32, (MAIN, tok), 0).astype(F32)
 
-    def pack(b, carry):
-        base = b * ns
+    def pack(q, carry):
+        base = q * ns
         hits, scales = [], []
         for u in range(ns):
-            row = jnp.broadcast_to(place_t[pl.ds(base + u, 1), :], (MAIN, tok))
-            wrow = jnp.broadcast_to(weight_t[pl.ds(base + u, 1), :], (MAIN, tok))
+            e = partner(base + u, True)
+            pk[pl.ds(base + u, 1), :] = place_t[pl.ds(e, 1), :]
+            wk[pl.ds(base + u, 1), :] = weight_t[pl.ds(e, 1), :]
+            row = jnp.broadcast_to(place_t[pl.ds(e, 1), :], (MAIN, tok))
+            wrow = jnp.broadcast_to(weight_t[pl.ds(e, 1), :], (MAIN, tok))
             same = row == slot_id
             hits.append(jnp.where(same, 1.0, 0.0))
             scales.append(jnp.sum(jnp.where(same, wrow, 0.0), axis=1, keepdims=True))
+        chunk = pl.ds(base, ns)
+        ninth = pk[chunk, :] == float(MAIN)
+        scale = jnp.sum(jnp.where(ninth, wk[chunk, :], 0.0), axis=1, keepdims=True)
+        pick = jnp.where(ninth, 1.0, 0.0).astype(BF16)
+        x = dot(pick, tokens[...])
+        g = dot(pick, grads[...]) * scale
+        for c in range(nc):
+            cols = slice(c * LANES, (c + 1) * LANES)
+            ovs[:, c, :] = x[:, cols]
+            ovs[:, nc + c, :] = g[:, cols]
+        send[chunk, 2 * nc] = ovs[...].astype(BF16)
         pick = jnp.concatenate(hits, axis=0)
         scale = jnp.concatenate(scales, axis=0)
-        pt[b] = pick.T.astype(BF16)
+        pt[q] = pick.T.astype(BF16)
         pick = pick.astype(BF16)
         x = dot(pick, tokens[...])
         g = dot(pick, grads[...]) * scale
         for c in range(nc):
             cols = slice(c * LANES, (c + 1) * LANES)
-            send[pl.ds(base, ns), c] = x[:, cols].reshape(ns, MAIN, LANES).astype(BF16)
-            send[pl.ds(base, ns), nc + c] = g[:, cols].reshape(ns, MAIN, LANES).astype(BF16)
+            send[chunk, c] = x[:, cols].reshape(ns, MAIN, LANES).astype(BF16)
+            send[chunk, nc + c] = g[:, cols].reshape(ns, MAIN, LANES).astype(BF16)
+
+        @pl.when(q == 0)
+        def _():
+            pltpu.make_async_copy(send.at[0], ga.at[0], a_r.at[0]).start()
+
+        def dispatch(k, carry):
+            dev = {"expert": partner(k, True)}
+            remote(send.at[k], ga.at[k], a_s.at[q], a_r.at[q], dev).start()
+            return carry
+
+        lax.fori_loop(jnp.maximum(base, 1), base + ns, dispatch, 0)
         return carry
 
     lax.fori_loop(0, nq, pack, 0)
-    same = place_t[...] == float(MAIN)
-    scale = jnp.sum(jnp.where(same, weight_t[...], 0.0), axis=1, keepdims=True)
-    pick = jnp.where(same, 1.0, 0.0)
-    pot[...] = pick.T.astype(BF16)
-    pick = pick.astype(BF16)
-    x = dot(pick, tokens[...])
-    g = dot(pick, grads[...]) * scale
-    for c in range(nc):
-        cols = slice(c * LANES, (c + 1) * LANES)
-        ovf[:, c, :] = x[:, cols]
-        ovf[:, nc + c, :] = g[:, cols]
-    send[:, 2 * nc] = ovf[...].astype(BF16)
-
-    pltpu.make_async_copy(send.at[me], ga.at[0], a_r.at[0]).start()
-
-    def dispatch(k, carry):
-        dest = lax.rem(me + lax.rem(k * STRIDE, n_e), n_e)
-        q = k // ns
-        remote(send.at[dest], ga.at[k], a_s.at[q], a_r.at[q], {"expert": dest}).start()
-        return carry
-
-    lax.fori_loop(1, n_e, dispatch, 0)
+    pot[...] = jnp.where(pk[...] == float(MAIN), 1.0, 0.0).T.astype(BF16)
 
     def at(q):
         return pl.ds(pl.multiple_of(q * rows, 16), rows)
@@ -231,16 +259,16 @@
 
         @pl.when(q == 0)
         def _():
-            pltpu.make_async_copy(back.at[0], ret.at[me], b_r).start()
+            pltpu.make_async_copy(back.at[0], ret.at[0], b_r.at[0]).start()
 
         def answer(k, carry):
-            dest = lax.rem(me + n_e - lax.rem(k * STRIDE, n_e), n_e)
-            remote(back.at[k], ret.at[me], b_s, b_r, {"expert": dest}).start()
+            dev = {"expert": partner(k, False)}
+            remote(back.at[k], ret.at[k], b_s, b_r.at[q], dev).start()
             return carry
 
         lax.fori_loop(jnp.maximum(base, 1), base + ns, answer, 0)
 
-    last = nq - max(1, nq // 4)
+    last = nq - 1
     middle = (last + 1) // 2
     ranges = [(0, middle), (middle, last)] if middle < last else [(0, last)]
 
@@ -280,7 +308,7 @@
 
         return carry
 
-    lax.fori_loop(0, nq + 4, step, 0)
+    lax.fori_loop(0, nq + 3, step, 0)
 
     outs = (o_gate, o_up, o_down)
 
@@ -299,6 +327,7 @@
     ]
     for copy in theirs:
         copy.start()
+    stage5(nq - 1)
     both, down = weight_grads(0, last, nq)
     dwo[:gu] = (acc[0, :gu] + both).astype(BF16)
     dwo[gu:] = (acc[0, gu:] + down).astype(BF16)
@@ -310,14 +339,16 @@
     for copy in mine:
         copy.start()
 
-    drain(ret, b_r)
+    total = [jnp.zeros((tok, LANES), F32) for c in range(nc)]
+    for q in range(nq):
+        chunk = slice(q * ns, (q + 1) * ns)
+        drain(ret.at[chunk], b_r.at[q])
+        for c in range(nc):
+            total[c] = total[c] + dot(pt[q], ret[chunk, c].reshape(ns * MAIN, LANES))
     ovf[...] = ret[:, nc].astype(F32)
     for c in range(nc):
-        total = dot(pot[...], ovf[:, c, :].astype(BF16))
-        for b in range(nq):
-            part = ret[pl.ds(b * ns, ns), c].reshape(ns * MAIN, LANES)
-            total = total + dot(pt[b], part)
-        o_tok[:, c * LANES : (c + 1) * LANES] = total.astype(BF16)
+        total[c] = total[c] + dot(pot[...], ovf[:, c, :].astype(BF16))
+        o_tok[:, c * LANES : (c + 1) * LANES] = total[c].astype(BF16)
 
     for swap in swaps:
         swap.wait_send()
@@ -363,10 +394,16 @@
     outs = pl.pallas_call(
         functools.partial(kernel, n_e, n_x, nq),
         out_shape=(jax.ShapeDtypeStruct((tok, feat), BF16), grad_shape, grad_shape, grad_shape),
-        in_specs=[vmem] * 4 + [hbm] * 3,
+        in_specs=[pl.BlockSpec(memory_space=pltpu.HBM)] * 7,
         out_specs=(vmem, hbm, hbm, hbm),
         scratch_shapes=[
+            pltpu.VMEM((tok, feat), BF16),
+            pltpu.VMEM((tok, feat), BF16),
+            pltpu.VMEM((routes.shape[1], tok), jnp.int32),
+            pltpu.VMEM((routes.shape[1], tok), F32),
             pltpu.VMEM((2, 3 * hid, two), BF16),
+            pltpu.VMEM((n_e, tok), F32),
+            pltpu.VMEM((n_e, tok), F32),
             pltpu.VMEM((n_e, tok), F32),
             pltpu.VMEM((n_e, tok), F32),
             pltpu.VMEM((nq, tok, ns * MAIN), BF16),
@@ -392,16 +429,17 @@
             pltpu.VMEM((2, 3 * hid, two), F32),
             pltpu.VMEM((3 * hid, two), BF16),
             pltpu.VMEM((3 * hid, two), BF16),
+            dma((4,)),
             dma((3, 2)),
             dma((3, 2)),
             dma((3, 2)),
         ]
         + [dma((nq,))] * 10
-        + [dma(()), dma(()), dma((3, 2)), dma((3, 2)), dma((3, 2))],
+        + [dma(()), dma((nq,)), dma((3, 2)), dma((3, 2)), dma((3, 2))],
         compiler_params=pltpu.CompilerParams(
             collective_id=0, has_side_effects=True, vmem_limit_bytes=VMEM_MIB * 1024 * 1024
         ),
-    )(tokens, out_grad, routes.T, combine.T, w_gate[0], w_up[0], w_down[0])
+    )(*[pltpu.with_memory_space_constraint(a, pltpu.HBM) for a in (tokens, out_grad, routes.T, combine.T, w_gate[0], w_up[0], w_down[0])])
     grad_tokens, grad_gate, grad_up, grad_down = outs
     return grad_tokens, grad_gate[None], grad_up[None], grad_down[None]
 

time: 158 us -> 149 us (0.943)
  the two profiles are of different devices: /device:TPU:64 before, /device:TPU:128 now
where the time goes in v3:
time: 149 us
  Pallas kernels  145 us (97%)
  local copies, waits for them, and re-layouts  3.29 us (2%)
    pallas_call x1, Pallas kernels, body(): pl.pallas_call(functools.partial(kernel, n_e, n_x, nq), out_shape=(jax.Sh...  145 us
    unnamed x4, local copies, waits for them, and re-layouts  3.29 us

profile of v3, /device:TPU:128, one launch (start us, length us, event | category | flops | bytes accessed | tf_op | source)
XLA Modules:
  0.0 149.3 jit_solution(12622315005231513324)
XLA Ops:
  0.6 145.3 %shard_map.102 = (bf16[128,512]{1,0:T(8,128)(2,1)S(1)}, bf16[192,2048]{1,0:T(8,128)(2,1)S(1)}, bf16[192,2048]{1,0:T(8,128)(2,1)S(1)}, bf16[192,2048]{1,0:T(8,128)(2,1)S(1)}) custom-call(bf16[128,512]{1,0:T(8,128)(2,1)} %tok_h.1, bf16[128,512]{1,0:T(8,128)(2,1)} %grad_h.1, s32[8,128]{1,0:T(8,128)} %bitcast.14, f32[8,128]{1,0:T(8,128)} %bitcast.15, ...), custom_call_target="tpu_custom_call" | custom-call | tf_op jit(solution)/shard_map/pallas_call | solution.py:394
  146.0 0.7 copy.15
  146.6 0.9 copy.16
  147.5 0.9 copy.17
  148.4 0.9 copy.18

commit v4 on v3

--- a/solution.py
+++ b/solution.py
@@ -12,7 +12,7 @@
 F32 = jnp.float32
 LANES = 128
 MAIN = 8
-STRIDE = 37
+STRIDE = 3
 SPAN = 8
 CHUNKS = 8
 VMEM_MIB = 48
@@ -66,8 +66,10 @@
     layers = n_e // (2 * span)
 
     def partner(k, ahead):
-        m = lax.rem(k * STRIDE, n_e)
-        step_c, step_y, step_z = lax.rem(m, 2), lax.rem(m // 2, span), m // (2 * span)
+        lo, hi = lax.rem(k, 2 * span), k // (2 * span)
+        step_c = lo // span
+        step_y = lax.rem(lo * STRIDE, span)
+        step_z = lax.rem(step_y + hi, layers)
         if not ahead:
             step_c, step_y, step_z = 2 - step_c, span - step_y, layers - step_z
         z = lax.rem(me // (2 * span) + step_z, layers)
@@ -439,7 +441,12 @@
         compiler_params=pltpu.CompilerParams(
             collective_id=0, has_side_effects=True, vmem_limit_bytes=VMEM_MIB * 1024 * 1024
         ),
-    )(*[pltpu.with_memory_space_constraint(a, pltpu.HBM) for a in (tokens, out_grad, routes.T, combine.T, w_gate[0], w_up[0], w_down[0])])
+    )(
+        *[
+            pltpu.with_memory_space_constraint(a, pltpu.HBM)
+            for a in (tokens, out_grad, routes.T, combine.T, w_gate[0], w_up[0], w_down[0])
+        ]
+    )
     grad_tokens, grad_gate, grad_up, grad_down = outs
     return grad_tokens, grad_gate[None], grad_up[None], grad_down[None]
 

time: 149 us -> 146 us (0.980)
  the two profiles are of different devices: /device:TPU:128 before, /device:TPU:131 now
where the time goes in v4:
time: 146 us
  Pallas kernels  142 us (97%)
  local copies, waits for them, and re-layouts  3.29 us (2%)
    pallas_call x1, Pallas kernels, body(): pl.pallas_call(functools.partial(kernel, n_e, n_x, nq), out_shape=(jax.Sh...  142 us
    unnamed x4, local copies, waits for them, and re-layouts  3.29 us

profile of v4, /device:TPU:131, one launch (start us, length us, event | category | flops | bytes accessed | tf_op | source)
XLA Modules:
  0.0 146.2 jit_solution(6871413973392107109)
XLA Ops:
  0.6 142.2 %shard_map.102 = (bf16[128,512]{1,0:T(8,128)(2,1)S(1)}, bf16[192,2048]{1,0:T(8,128)(2,1)S(1)}, bf16[192,2048]{1,0:T(8,128)(2,1)S(1)}, bf16[192,2048]{1,0:T(8,128)(2,1)S(1)}) custom-call(bf16[128,512]{1,0:T(8,128)(2,1)} %tok_h.1, bf16[128,512]{1,0:T(8,128)(2,1)} %grad_h.1, s32[8,128]{1,0:T(8,128)} %bitcast.14, f32[8,128]{1,0:T(8,128)} %bitcast.15, ...), custom_call_target="tpu_custom_call" | custom-call | tf_op jit(solution)/shard_map/pallas_call | solution.py:396
  142.9 0.7 copy.15
  143.5 0.9 copy.16
  144.4 0.9 copy.17
  145.3 0.9 copy.18

commit v5 on v4

--- a/solution.py
+++ b/solution.py
@@ -12,6 +12,7 @@
 F32 = jnp.float32
 LANES = 128
 MAIN = 8
+HALF = 4
 STRIDE = 3
 SPAN = 8
 CHUNKS = 8
@@ -66,8 +67,8 @@
     layers = n_e // (2 * span)
 
     def partner(k, ahead):
-        lo, hi = lax.rem(k, 2 * span), k // (2 * span)
-        step_c = lo // span
+        lo, hi = lax.rem(k, span), lax.rem(k // span, layers)
+        step_c = k // (span * layers)
         step_y = lax.rem(lo * STRIDE, span)
         step_z = lax.rem(step_y + hi, layers)
         if not ahead:
@@ -245,19 +246,24 @@
         part = dot(mine, wt[0, :gu, feat:]) + dot(theirs, wt[1, :gu, feat:])
         ys[at(q), :] = part.astype(BF16)
         remote(ys.at[at(q)], yr.at[at(q)], y_s.at[q], y_r.at[q], on_a).start()
+
+    def stage4_own(q):
+        mine = tm[at(q), :gu]
+        theirs = tp[at(q), :gu]
         y_own[at(q), :] = dot(mine, wt[0, :gu, :feat]) + dot(theirs, wt[1, :gu, :feat])
 
     def stage5(q):
         base = q * ns
         drain(yr.at[at(q)], y_r.at[q])
         slot = y_own[at(q), :] + yr[at(q), :].astype(F32)
-        ovs[...] = jnp.zeros_like(ovs)
         for c in range(nc):
             cols = slice(c * LANES, (c + 1) * LANES)
             main = slot[: ns * MAIN, cols].reshape(ns, MAIN, LANES)
-            back[pl.ds(base, ns), c] = main.astype(BF16)
+            for h in range(2):
+                half = main[:, h * HALF : (h + 1) * HALF]
+                back[pl.ds(base, ns), 2 * c + h] = half.astype(BF16)
             ovs[:, c, :] = slot[ns * MAIN :, cols]
-        back[pl.ds(base, ns), nc] = ovs[...].astype(BF16)
+        back[pl.ds(base, ns), 2 * nc] = ovs[:, :HALF].astype(BF16)
 
         @pl.when(q == 0)
         def _():
@@ -294,12 +300,14 @@
             @pl.when(jnp.logical_and(q >= 0, q < nq))
             def _():
                 stage(q)
+                if stage is stage4:
+                    stage4_own(q)
 
         for n, (first, stop) in enumerate(ranges):
 
             @pl.when(t - 3 == stop - 1)
             def _():
-                for block in range(2):
+                for block in (0, 1) if n == 0 else (1,):
                     both, down = weight_grads(block, first, stop)
                     if n == 0:
                         acc[block, :gu] = both
@@ -310,7 +318,8 @@
 
         return carry
 
-    lax.fori_loop(0, nq + 3, step, 0)
+    lax.fori_loop(0, nq + 2, step, 0)
+    stage4(nq - 1)
 
     outs = (o_gate, o_up, o_down)
 
@@ -329,8 +338,10 @@
     ]
     for copy in theirs:
         copy.start()
+    stage4_own(nq - 1)
+    stage5(nq - 2)
     stage5(nq - 1)
-    both, down = weight_grads(0, last, nq)
+    both, down = weight_grads(0, ranges[0][1], nq)
     dwo[:gu] = (acc[0, :gu] + both).astype(BF16)
     dwo[gu:] = (acc[0, gu:] + down).astype(BF16)
     mine = [
@@ -346,8 +357,11 @@
         chunk = slice(q * ns, (q + 1) * ns)
         drain(ret.at[chunk], b_r.at[q])
         for c in range(nc):
-            total[c] = total[c] + dot(pt[q], ret[chunk, c].reshape(ns * MAIN, LANES))
-    ovf[...] = ret[:, nc].astype(F32)
+            for h in range(2):
+                ovs[:, h * HALF : (h + 1) * HALF] = ret[chunk, 2 * c + h].astype(F32)
+            part = ovs[...].reshape(ns * MAIN, LANES).astype(BF16)
+            total[c] = total[c] + dot(pt[q], part)
+    ovf[:, :HALF] = ret[:, 2 * nc].astype(F32)
     for c in range(nc):
         total[c] = total[c] + dot(pot[...], ovf[:, c, :].astype(BF16))
         o_tok[:, c * LANES : (c + 1) * LANES] = total[c].astype(BF16)
@@ -426,8 +440,8 @@
             pltpu.VMEM((slots, feat), F32),
             pltpu.VMEM((slots, feat), BF16),
             pltpu.VMEM((slots, feat), BF16),
-            pltpu.VMEM((n_e, nc + 1, MAIN, LANES), BF16),
-            pltpu.VMEM((n_e, nc + 1, MAIN, LANES), BF16),
+            pltpu.VMEM((n_e, 2 * nc + 1, HALF, LANES), BF16),
+            pltpu.VMEM((n_e, 2 * nc + 1, HALF, LANES), BF16),
             pltpu.VMEM((2, 3 * hid, two), F32),
             pltpu.VMEM((3 * hid, two), BF16),
             pltpu.VMEM((3 * hid, two), BF16),

time: 146 us -> 155 us (1.062)
  the two profiles are of different devices: /device:TPU:131 before, /device:TPU:1 now
where the time goes in v5:
time: 155 us; the launch traced here: 153 us
  Pallas kernels  149 us (96%)
  local copies, waits for them, and re-layouts  3.29 us (2%)
    pallas_call x1, Pallas kernels, body(): pl.pallas_call(functools.partial(kernel, n_e, n_x, nq), out_shape=(jax.Sh...  149 us
    unnamed x4, local copies, waits for them, and re-layouts  3.29 us

profile of v5, /device:TPU:1, one launch (start us, length us, event | category | flops | bytes accessed | tf_op | source)
XLA Modules:
  0.0 152.7 jit_solution(14064351275541736855)
XLA Ops:
  0.6 148.8 %shard_map.102 = (bf16[128,512]{1,0:T(8,128)(2,1)S(1)}, bf16[192,2048]{1,0:T(8,128)(2,1)S(1)}, bf16[192,2048]{1,0:T(8,128)(2,1)S(1)}, bf16[192,2048]{1,0:T(8,128)(2,1)S(1)}) custom-call(bf16[128,512]{1,0:T(8,128)(2,1)} %tok_h.1, bf16[128,512]{1,0:T(8,128)(2,1)} %grad_h.1, s32[8,128]{1,0:T(8,128)} %bitcast.14, f32[8,128]{1,0:T(8,128)} %bitcast.15, ...), custom_call_target="tpu_custom_call" | custom-call | tf_op jit(solution)/shard_map/pallas_call | solution.py:410
  149.4 0.7 copy.15
  150.1 0.9 copy.16
  151.0 0.9 copy.17
  151.8 0.9 copy.18
